TPU v7x, 32 devices: a whole 2x2x4 slice. The times are simulated.
32 devices in a mesh: dp: 8 (over y, x, core), mp: 4 (over z).
Axes of the slice: x: 2, y: 2, z: 4, core: 2. Of those that a mesh axis runs over, the one named last changes fastest.
Arguments:
- patches: bfloat16 [8192, 768], P('dp'), may hold values from -6 to 6
- attention_gain: bfloat16 [768], replicated, may hold values from 0.5 to 1.5
- query_weight: bfloat16 [768, 768], P(None, 'mp'), may hold values from -0.0390625 to 0.0390625
- key_weight: bfloat16 [768, 768], P(None, 'mp'), may hold values from -0.3125 to 0.3125
- value_weight: bfloat16 [768, 768], P(None, 'mp'), may hold values from -0.21875 to 0.21875
- output_weight: bfloat16 [768, 768], P('mp'), may hold values from -0.875 to 0.875
- feedforward_gain: bfloat16 [768], replicated, may hold values from 0.5 to 1.5
- gate_weight: bfloat16 [768, 2048], P(None, 'mp'), may hold values from -0.21875 to 0.21875
- up_weight: bfloat16 [768, 2048], P(None, 'mp'), may hold values from -0.21875 to 0.21875
- down_weight: bfloat16 [2048, 768], P('mp'), may hold values from -0.25 to 0.25
- cotangent: bfloat16 [8192, 768], P('dp'), may hold values from -6 to 6
- grid_extent: int32 [8, 2], P('dp'), may hold values from 16 to 32, as said below
Outputs:
- layer_output: bfloat16 [8192, 768], P('dp')
- input_grad: float32 [8192, 768], P('dp')
- attention_grad: float32 [768], P('dp')
- query_grad: float32 [768, 768], P('dp', 'mp')
- key_grad: float32 [768, 768], P('dp', 'mp')
- value_grad: float32 [768, 768], P('dp', 'mp')
- output_grad: float32 [768, 768], P('mp', 'dp')
- feedforward_grad: float32 [768], P('dp')
- gate_grad: float32 [768, 2048], P('dp', 'mp')
- up_grad: float32 [768, 2048], P('dp', 'mp')
- down_grad: float32 [2048, 768], P('mp', 'dp')
Inputs may be any that keep to these rules, and one draw needn't show every extreme that they name: `grid_extent`: chart 0 has all 32 rows and columns.
All inputs are finite; a program needn't handle non-finite values.
Results may differ from a plain program's by a relative error of at most 0.015.
Values may be sent and summed in bfloat16 or wider, within the bound.
A program may use at most 128 MiB of HBM per device.

v0:
```python
import functools

import jax
import jax.numpy as jnp
from jax import lax
from jax.experimental import pallas as pl
from jax.experimental.pallas import tpu as pltpu
from jax.sharding import PartitionSpec as P

HEAD = 64
EPSILON = 1e-06
MASKED = -1000000000.0
MESH = pl.DeviceIdType.MESH
f32 = jnp.float32
bf16 = jnp.bfloat16
GROUP = 8
VMEM_LIMIT = 61 << 20


def dot(left, right, left_dim, right_dim):
    return lax.dot_general(
        left, right, (((left_dim,), (right_dim,)), ((), ())), preferred_element_type=f32
    )


def flip(value, bits):
    result = value
    for bit in (1, 2, 4):
        if bits & bit:
            result = result + bit - 2 * bit * ((value // bit) % 2)
    return result


def cross(value, mask):
    low = (value + mask) % 2
    return low + 2 * ((value // 2 + mask // 2) % 2)


def aligned(value, multiple):
    return pl.multiple_of(value, multiple)


class Gather:
    KINDS = 5

    def __init__(self, sources, places, send_z, recv_z, send_x, recv_x, send_c, recv_c):
        self.dp, self.mp = lax.axis_index("dp"), lax.axis_index("mp")
        self.core = self.dp % 2
        self.chip = (self.dp // 2) % 4
        self.sources, self.places = sources, places
        self.sems = (send_z, recv_z, send_x, recv_x, send_c, recv_c)
        self.sends = []

    def part(self, ref, lead, quarter, half):
        rows, columns = ref.shape[-2] // 4, ref.shape[-1] // 2
        window = (
            pl.ds(aligned(quarter * rows, 16), rows),
            pl.ds(aligned(half * columns, 128), columns),
        )
        middle = (slice(None),) * (len(ref.shape) - 2 - len(lead))
        return ref.at[(*lead, *middle, *window)]

    def place(self, kind, shard, quarter, half):
        return self.part(self.places[kind], (shard,), quarter, half)

    def copy(self, source, target, send, recv, dp, mp):
        return pltpu.make_async_remote_copy(
            src_ref=source,
            dst_ref=target,
            send_sem=send,
            recv_sem=recv,
            device_id=(dp, mp),
            device_id_type=MESH,
        )

    def start(self, make, *which):
        make(*which).start()
        self.sends.append((make, which))

    def arrived(self, target, send, recv):
        self.copy(target, target, send, recv, self.dp, self.mp).wait_recv()

    def along_mp(self, kind, k):
        send_z, recv_z = self.sems[:2]
        target = self.place(kind, self.mp, self.chip, self.core)
        source = target
        if self.sources[kind] is not None:
            source = self.part(self.sources[kind], (), self.chip, self.core)
        peer = flip(self.mp, k)
        return self.copy(source, target, send_z.at[kind, k], recv_z.at[kind, k], self.dp, peer)

    def to_core(self, kind, k, j):
        piece = self.place(kind, flip(self.mp, k), flip(self.chip, j), self.core)
        send_c, recv_c = self.sems[4:]
        peer = flip(self.dp, 1)
        return self.copy(piece, piece, send_c.at[kind, k, j], recv_c.at[kind, k, j], peer, self.mp)

    def to_chip(self, kind, k, j):
        send_x, recv_x = self.sems[2:4]
        quarter, peer = self.chip, flip(self.dp, 2 * j)
        if j == 3:
            from_y, from_x = flip(self.chip, 2), flip(self.chip, 1)
            to_x, to_y = flip(self.dp, 2), flip(self.dp, 4)
            quarter = from_y + self.core * (from_x - from_y)
            peer = to_x + self.core * (to_y - to_x)
        piece = self.place(kind, flip(self.mp, k), quarter, self.core)
        return self.copy(piece, piece, send_x.at[kind, k, j], recv_x.at[kind, k, j], peer, self.mp)

    def to_chips(self, kind, k):
        send_z, recv_z = self.sems[:2]
        piece = self.place(kind, flip(self.mp, k), self.chip, self.core)
        self.arrived(piece, send_z.at[kind, k], recv_z.at[kind, k])
        self.start(self.to_chip, kind, k, 1)
        self.start(self.to_chip, kind, k, 2)
        self.start(self.to_core, kind, k, 0)

    def to_corner(self, kind, k):
        send_x, recv_x = self.sems[2:4]
        for j in (1, 2):
            piece = self.place(kind, flip(self.mp, k), flip(self.chip, j), self.core)
            self.arrived(piece, send_x.at[kind, k, j], recv_x.at[kind, k, j])
        self.start(self.to_chip, kind, k, 3)
        self.start(self.to_core, kind, k, 1)
        self.start(self.to_core, kind, k, 2)

    def last_core(self, kind, k):
        send_x, recv_x = self.sems[2:4]
        piece = self.place(kind, flip(self.mp, k), flip(self.chip, 3), self.core)
        self.arrived(piece, send_x.at[kind, k, 3], recv_x.at[kind, k, 3])
        self.start(self.to_core, kind, k, 3)

    def settled(self, kind, k):
        send_c, recv_c = self.sems[4:]
        for j in range(4):
            piece = self.place(kind, flip(self.mp, k), flip(self.chip, j), 1 - self.core)
            self.arrived(piece, send_c.at[kind, k, j], recv_c.at[kind, k, j])

    def schedule(self, jobs, window=8, start=3.0, pace=3.2, lags=(6.0, 12.0, 14.0)):
        for job in jobs[:window]:
            self.start(self.along_mp, *job)

        def first(i):
            self.to_chips(*jobs[i])
            if i + window < len(jobs):
                self.start(self.along_mp, *jobs[i + window])

        steps = []
        clock = start
        for i, job in enumerate(jobs):
            clock += 0.37 * pace if job[0] == 1 else pace
            steps.append((clock, functools.partial(first, i), job, False))
            later = (self.to_corner, self.last_core, self.settled)
            for lag, step in zip(lags, later):
                steps.append((clock + lag, functools.partial(step, *job), job, step == later[-1]))
        return sorted(steps, key=lambda step: step[0])

    def finish(self):
        for make, which in self.sends:
            make(*which).wait_send()


def announce(devices):
    semaphore = pltpu.get_barrier_semaphore()
    for device in devices:
        pl.semaphore_signal(semaphore, inc=1, device_id=device, device_id_type=MESH)
    return semaphore


def row_keep(count, first, rows):
    return lax.broadcasted_iota(jnp.int32, (rows, 1), 0) + first < count


def project(weights_ref, normed_ref, out_ref, shard):
    parts, features, depth = weights_ref.shape[1:]
    rows = normed_ref.shape[0]
    block = 512

    def step(i, _):
        at = pl.ds(aligned(i * block, block), block)
        weights = weights_ref[shard].reshape(parts * features, depth)
        out_ref[shard, :, at] = dot(weights, normed_ref[at, :], 1, 1).astype(bf16)
        return 0

    lax.fori_loop(0, rows // block, step, 0)


def attend(qkv_ref, shard, head, count, probs_ref, context_ref, scale_ref, scores, keys, local_heads, pause):
    rows = qkv_ref.shape[2]
    width = local_heads * HEAD
    block, chunk, group = 256, 128, 64
    at = pl.ds(aligned(head * HEAD, HEAD), HEAD)
    number = shard * local_heads + head
    context_at = pl.ds(aligned(number * HEAD, HEAD), HEAD)
    masked = jnp.where(row_keep(count, 0, rows), 0.0, MASKED)
    first_lane = lax.broadcasted_iota(jnp.int32, (rows, HEAD), 1) == 0
    keys[:, :HEAD] = qkv_ref[shard, pl.ds(aligned(width + head * HEAD, HEAD), HEAD), :].T
    keys[:, HEAD:] = jnp.where(first_lane, masked, 0.0).astype(bf16)
    queries = jnp.concatenate([qkv_ref[shard, at, :], jnp.ones((HEAD, rows), bf16)], axis=0)
    values = qkv_ref[shard, pl.ds(aligned(2 * width + head * HEAD, HEAD), HEAD), :]
    values = jnp.concatenate([values, jnp.ones((16, rows), bf16)], axis=0)
    blocks = rows // block
    highest = None
    for i in range(blocks + 1):
        ahead = None
        for first in range(0, rows, chunk):
            part = slice(first, first + chunk)
            if i < blocks:
                product = dot(keys[part, :], queries[:, i * block : (i + 1) * block], 1, 0)
                scores[i % 2, part, :] = product
                top = jnp.max(product.reshape(chunk // group, group, block), axis=0)
                ahead = top if ahead is None else jnp.maximum(ahead, top)
            if i > 0:
                weights = jnp.exp(scores[(i - 1) % 2, part, :] - highest)
                probs_ref[part, (i - 1) * block : i * block] = weights.astype(bf16)
        if i > 0:
            columns = slice((i - 1) * block, i * block)
            context = dot(values, probs_ref[:, columns], 1, 0)
            scale = 1.0 / context[HEAD : HEAD + 1]
            context_ref[context_at, columns] = (context[:HEAD] * scale).astype(bf16)
            scale_ref[number, :, columns] = scale
        if i < blocks:
            highest = jnp.max(ahead, axis=0, keepdims=True)
            pause(i)


def gelu_parts(gate):
    root = 0.7978845608028654
    square = gate * gate
    bend = jnp.tanh(gate * (root + (root * 0.044715) * square))
    half = 0.5 + 0.5 * bend
    slope = half + (0.5 * gate) * (1.0 - bend * bend) * (root + (3 * root * 0.044715) * square)
    return gate * half, slope


def attend_back(qkv_ref, grad_ref, shard, head, probs, context_back, delta, score_back, local_heads):
    rows = qkv_ref.shape[2]
    width = local_heads * HEAD
    block = 256
    head_at = pl.ds(aligned(head * HEAD, HEAD), HEAD)
    key_at = pl.ds(aligned(width + head * HEAD, HEAD), HEAD)
    value_at = pl.ds(aligned(2 * width + head * HEAD, HEAD), HEAD)
    number = shard * local_heads + head
    upstream = context_back[pl.ds(aligned(number * HEAD, HEAD), HEAD), :]
    queries, keys = qkv_ref[shard, head_at, :], qkv_ref[shard, key_at, :]
    high = delta[number].astype(bf16)
    low = (delta[number] - high.astype(f32)).astype(bf16)
    right = jnp.concatenate([upstream, high, low, jnp.zeros((14, rows), bf16)], axis=0)
    lane = lax.broadcasted_iota(jnp.int32, (rows, 16), 1)
    minus = jnp.where(lane < 2, -1.0, 0.0).astype(bf16)
    left = jnp.concatenate([qkv_ref[shard, value_at, :].T, minus], axis=1)
    for first in range(0, rows, block):
        part = slice(first, first + block)
        for i in range(0, rows, block):
            columns = slice(i, i + block)
            change = dot(left[part], right[:, columns], 1, 0)
            score_back[part, columns] = (probs[part, columns].astype(f32) * change).astype(bf16)
        grad_ref[shard, value_at, part] = dot(upstream, probs[part, :], 1, 1).astype(bf16)
        grad_ref[shard, key_at, part] = dot(queries, score_back[part, :], 1, 1).astype(bf16)
    grad_ref[shard, head_at, :] = dot(keys, score_back[...], 1, 0).astype(bf16)


class Reduce:
    def __init__(self, local, from_core, from_chips, total, sems):
        self.local, self.from_core = local, from_core
        self.from_chips, self.total, self.sems = from_chips, total, sems
        self.dp, self.mp = lax.axis_index("dp"), lax.axis_index("mp")
        self.core, self.chip = self.dp % 2, (self.dp // 2) % 4

    def copy(self, j):
        if j == 0:
            source, target, peer = self.local.at[:, 1 - self.core], self.from_core, flip(self.dp, 1)
        else:
            source, target = self.local.at[flip(self.chip, j), self.core], self.from_chips.at[j - 1]
            peer = flip(self.dp, 2 * j)
        return pltpu.make_async_remote_copy(
            src_ref=source,
            dst_ref=target,
            send_sem=self.sems.at[0, j],
            recv_sem=self.sems.at[1, j],
            device_id=(peer, self.mp),
            device_id_type=MESH,
        )

    def begin(self):
        self.copy(0).start()

    def middle(self):
        self.copy(0).wait()
        for j in (1, 2, 3, 0):
            chip = flip(self.chip, j)
            part = self.local[chip, self.core].astype(f32) + self.from_core[chip].astype(f32)
            if j == 0:
                self.total[...] = part
            else:
                self.local[chip, self.core] = part.astype(bf16)
                self.copy(j).start()

    def end(self):
        for j in (1, 2, 3):
            self.copy(j).wait()
        first, second, third = (self.from_chips[i].astype(f32) for i in range(3))
        self.total[...] += first + second + third


def main_kernel(
    extent,
    inputs,
    first_gain,
    second_gain,
    upstream,
    query_source,
    key_source,
    value_source,
    output_source,
    gate_source,
    up_source,
    down_source,
    layer_output,
    probs_out,
    grads_out,
    weights_out,
    hidden_out,
    wide_total,
    narrow_total,
    gains_total,
    attention_weights,
    output_weights,
    gate_weights,
    up_weights,
    down_weights,
    qkv,
    context,
    normed_one,
    normed_two,
    out_low,
    hidden,
    scale,
    delta,
    context_back,
    wide_grad,
    narrow_grad,
    wide_core,
    wide_chips,
    narrow_core,
    narrow_chips,
    gains_own,
    gains_in,
    own_weights,
    local_sem,
    probs_sem,
    out_sem,
    grads_sem,
    wide_sem,
    narrow_sem,
    gains_sem,
    send_z,
    recv_z,
    send_x,
    recv_x,
    send_c,
    recv_c,
):
    dp, mp = lax.axis_index("dp"), lax.axis_index("mp")
    shards = attention_weights.shape[0]
    rows, depth = inputs.shape
    features = output_weights.shape[1]
    units = gate_weights.shape[2]
    local_heads = features // HEAD
    heads = shards * local_heads
    count = extent[0, 0] * extent[0, 1]
    block = 256
    blocks = rows // block

    def each_block(step):
        def run(i, _):
            step(i * block, pl.ds(aligned(i * block, block), block))
            return 0

        lax.fori_loop(0, blocks, run, 0)

    sources = (None, output_source, gate_source, up_source, down_source)
    places = (attention_weights, output_weights, gate_weights, up_weights, down_weights)
    owned = [
        pltpu.make_async_copy(source, place.at[mp], local_sem.at[i])
        for i, (source, place) in enumerate(zip(sources[1:], places[1:]))
    ]
    owned.append(pltpu.make_async_copy(upstream, out_low, local_sem.at[4]))
    turned = [
        pltpu.make_async_copy(source, attention_weights.at[mp, i], local_sem.at[5 + i])
        for i, source in enumerate((query_source, key_source, value_source))
    ]
    peers = [(flip(dp, j), mp) for j in range(1, GROUP)]
    peers += [(dp, flip(mp, k)) for k in range(1, shards)]
    semaphore = announce(peers)
    for copy in turned + owned:
        copy.start()
    for copy in turned:
        copy.wait()
    own_weights[...] = attention_weights[mp].reshape(3 * features, depth).T
    pl.semaphore_wait(semaphore, len(peers))
    gather = Gather(sources, places, send_z, recv_z, send_x, recv_x, send_c, recv_c)
    jobs = [(kind, k) for kind in (0, 1) for k in range(1, shards)]
    jobs += [(kind, k) for k in range(1, shards) for kind in (2, 3, 4)]
    steps = gather.schedule(jobs)
    position = [0]
    clock = [0.0]

    def take(stop):
        chosen = steps[position[0] : stop]
        position[0] = max(position[0], stop)
        return chosen

    def due(spent):
        clock[0] += spent
        return take(sum(step[0] <= clock[0] for step in steps))

    def needed(job):
        where = [i for i, step in enumerate(steps) if step[3] and step[2] == job][0]
        clock[0] = max(clock[0], steps[where][0])
        return take(where + 1)

    def carry_out(chosen):
        for step in chosen:
            step[1]()

    def carry_out_at(index, plan):
        for number, chosen in plan.items():
            if chosen:
                pl.when(index == number)(functools.partial(carry_out, chosen))

    def gain_of(ref):
        return ref[...].astype(f32).reshape(1, depth)

    def normalise(first, at):
        values = inputs[at, :].astype(f32)
        root = lax.rsqrt(jnp.mean(values * values, axis=-1, keepdims=True) + EPSILON)
        normed_one[at, :] = (values * root * gain_of(first_gain)).astype(bf16)

    each_block(normalise)
    carry_out(due(1.5))

    def join(first, at):
        every_output = output_weights[...].reshape(depth, depth)
        values = inputs[at, :].astype(f32) + dot(context[:, at], every_output, 0, 0)
        hidden[at, :] = values
        root = lax.rsqrt(jnp.mean(values * values, axis=-1, keepdims=True) + EPSILON)
        normed_two[at, :] = (values * root * gain_of(second_gain)).astype(bf16)
        out_low[at, :] = jnp.where(row_keep(count, first, block), out_low[at, :], jnp.zeros((), bf16))

    def attention(probs, scores, keys):
        def probs_copy(slot, number):
            return pltpu.make_async_copy(probs.at[slot], probs_out.at[number], probs_sem.at[slot])

        shard_plan, project_plan, block_plans = {}, {}, [{} for _ in range(blocks)]
        for i in range(heads):
            if i % local_heads == 0:
                shard_plan[i] = needed((0, i // local_heads)) if i > 0 else []
                project_plan[i] = due(1.8)
            for plan in block_plans:
                plan[i] = due(0.4)

        def step(i, _):
            shard, head = cross(mp, i // local_heads), i % local_heads
            number = shard * local_heads + head

            @pl.when(head == 0)
            def _():
                carry_out_at(i, shard_plan)
                project(attention_weights, normed_one, qkv, shard)
                carry_out_at(i, project_plan)

            @pl.when(i >= 2)
            def _():
                probs_copy(i % 2, number).wait()

            attend(
                qkv,
                shard,
                head,
                count,
                probs.at[i % 2],
                context,
                scale,
                scores,
                keys,
                local_heads,
                lambda at: carry_out_at(i, block_plans[at]),
            )
            probs_copy(i % 2, number).start()
            return 0

        lax.fori_loop(0, heads, step, 0)
        pltpu.make_async_copy(attention_weights, weights_out, out_sem.at[0]).start()
        owned[0].wait()
        owned[4].wait()
        for k in range(1, shards):
            carry_out(needed((1, k)))
        each_block(join)
        carry_out(due(2.4))
        for slot in range(2):
            probs_copy(slot, 0).wait()

    pl.run_scoped(
        attention,
        pltpu.VMEM((2, rows, rows), bf16),
        pltpu.VMEM((2, rows, block), f32),
        pltpu.VMEM((rows, 2 * HEAD), bf16),
    )

    slices = wide_grad.shape[:3]
    wide = Reduce(wide_grad, wide_core, wide_chips, wide_total, wide_sem)
    narrow = Reduce(narrow_grad, narrow_core, narrow_chips, narrow_total, narrow_sem)

    def feed_forward(forward_sum, back_sum, mixed_own, gate_own, up_own):
        def feed(shard, k):
            def step(first, at):
                normed, low = normed_two[at, :], out_low[at, :]
                gate = dot(normed, gate_weights[shard], 1, 0)
                up = dot(normed, up_weights[shard], 1, 0)
                mixed_back = dot(low, down_weights[shard], 1, 1)
                bent, slope = gelu_parts(gate)
                mixed = (bent * up).astype(bf16)
                gate_back = (mixed_back * up * slope).astype(bf16)
                up_back = (mixed_back * bent).astype(bf16)
                ahead = dot(mixed, down_weights[shard], 1, 0)
                back = dot(gate_back, gate_weights[shard], 1, 1)
                back = back + dot(up_back, up_weights[shard], 1, 1)
                if k == 0:
                    mixed_own[at, :] = mixed
                    gate_own[at, :] = gate_back
                    up_own[at, :] = up_back
                    forward_sum[at, :] = ahead
                    back_sum[at, :] = back
                else:
                    forward_sum[at, :] += ahead
                    back_sum[at, :] += back

            plan = {i: due(1.5) for i in range(blocks)}

            def run(i, _):
                step(i * block, pl.ds(aligned(i * block, block), block))
                carry_out_at(i, plan)
                return 0

            lax.fori_loop(0, blocks, run, 0)

        for k in range(shards):
            if k == 0:
                for copy in owned[1:4]:
                    copy.wait()
            else:
                for kind in (2, 3, 4):
                    carry_out(needed((kind, k)))
            if k == shards - 1:
                carry_out(take(len(steps)))
                wide.middle()
            feed(flip(mp, k), k)
            if k == 0:
                pairs = ((normed_two, gate_own), (normed_two, up_own), (out_low, mixed_own))
                for i, (left, right) in enumerate(pairs):
                    part = dot(left[...], right[...], 0, 0).astype(bf16)
                    wide_grad[:, :, :, i * units : (i + 1) * units] = part.reshape(*slices, units)
                    carry_out(due(0.9))
                wide.begin()

        def close(first, at):
            keep = row_keep(count, first, block)
            values, back = hidden[at, :], back_sum[at, :]
            out_back = out_low[at, :].astype(f32)
            out_low[at, :] = jnp.where(keep, values + forward_sum[at, :], 0.0).astype(bf16)
            root = lax.rsqrt(jnp.mean(values * values, axis=-1, keepdims=True) + EPSILON)
            scaled = gain_of(second_gain) * back
            mean = jnp.mean(scaled * values, axis=-1, keepdims=True)
            result = out_back + root * scaled - values * (root * root * root * mean)
            hidden[at, :] = result
            normed_two[at, :] = result.astype(bf16)

        each_block(close)

    pl.run_scoped(
        feed_forward,
        pltpu.VMEM((rows, depth), f32),
        pltpu.VMEM((rows, depth), f32),
        pltpu.VMEM((rows, units), bf16),
        pltpu.VMEM((rows, units), bf16),
        pltpu.VMEM((rows, units), bf16),
    )
    pltpu.make_async_copy(out_low, layer_output, out_sem.at[1]).start()
    pltpu.make_async_copy(hidden, hidden_out, out_sem.at[2]).start()
    hidden_low = normed_two

    def context_step(first, at):
        every_output = output_weights[...].reshape(depth, depth)
        back = dot(every_output, hidden_low[at, :], 1, 1).reshape(heads, HEAD, block)
        low = (back * scale[:, :, at]).astype(bf16)
        context_back[:, at] = low.reshape(depth, block)
        ahead = context[:, at].reshape(heads, HEAD, block).astype(f32)
        delta[:, :, at] = jnp.sum(low.astype(f32) * ahead, axis=1, keepdims=True)

    each_block(context_step)

    def gains_copy(k):
        return pltpu.make_async_remote_copy(
            src_ref=gains_own,
            dst_ref=gains_in.at[k - 1],
            send_sem=gains_sem.at[0, k],
            recv_sem=gains_sem.at[1, k],
            device_id=(dp, flip(mp, k)),
            device_id_type=MESH,
        )

    def gains():
        piece = gains_own.shape[0]
        at = pl.ds(aligned((dp % GROUP) * piece, 32), piece)
        second = gate_weights[mp, at, :].astype(f32) * wide_total[:, :units]
        second = second + up_weights[mp, at, :].astype(f32) * wide_total[:, units : 2 * units]
        first = own_weights[at, :].astype(f32) * narrow_total[:, : 3 * features]
        lane = lax.broadcasted_iota(jnp.int32, gains_own.shape, 1)
        first = jnp.sum(first, axis=1, keepdims=True)
        second = jnp.sum(second, axis=1, keepdims=True)
        gains_own[...] = jnp.where(lane == 0, first, jnp.where(lane == 1, second, 0.0))
        for k in range(1, shards):
            gains_copy(k).start()

    def attention_back(probs, score_back, grads):
        def fetch(i):
            number = cross(mp, i // local_heads) * local_heads + i % local_heads
            return pltpu.make_async_copy(probs_out.at[number], probs.at[i % 2], probs_sem.at[i % 2])

        def keep_grads(shard, k):
            return pltpu.make_async_copy(grads.at[shard], grads_out.at[shard], grads_sem.at[k])

        def step(i, _):
            k, head = i // local_heads, i % local_heads
            shard = cross(mp, k)
            fetch(i).wait()

            @pl.when(i + 1 < heads)
            def _():
                fetch(i + 1).start()

            attend_back(
                qkv,
                grads,
                shard,
                head,
                probs.at[i % 2],
                context_back,
                delta,
                score_back,
                local_heads,
            )

            @pl.when(head == local_heads - 1)
            def _():
                keep_grads(shard, k).start()

            @pl.when(i == local_heads - 1)
            def _():
                own = context[pl.ds(aligned(mp * features, HEAD), features), :]
                part = jnp.concatenate(
                    [dot(grads[mp], normed_one[...], 1, 0), dot(own, hidden_low[...], 1, 0)], axis=0
                )
                narrow_grad[...] = part.T.astype(bf16).reshape(narrow_grad.shape)
                narrow.begin()

            @pl.when(i == local_heads)
            def _():
                narrow.middle()

            @pl.when(i == heads - 5)
            def _():
                wide.end()

            @pl.when(i == heads - 3)
            def _():
                narrow.end()
                gains()

            return 0

        fetch(0).start()
        lax.fori_loop(0, heads, step, 0)
        for k in range(shards):
            keep_grads(flip(mp, k), k).wait()

    pl.run_scoped(
        attention_back,
        pltpu.VMEM((2, rows, rows), bf16),
        pltpu.VMEM((rows, rows), bf16),
        pltpu.VMEM((shards, 3 * features, rows), bf16),
    )
    for k in range(1, shards):
        gains_copy(k).wait()
    gains_total[...] = (gains_own[...] + gains_in[0]) + (gains_in[1] + gains_in[2])
    pltpu.make_async_copy(attention_weights, weights_out, out_sem.at[0]).wait()
    pltpu.make_async_copy(out_low, layer_output, out_sem.at[1]).wait()
    pltpu.make_async_copy(hidden, hidden_out, out_sem.at[2]).wait()
    gather.finish()


def close_kernel(
    grads,
    weights,
    hidden_back,
    inputs,
    first_gain,
    layer_in,
    wide_total,
    narrow_total,
    input_grad,
    layer_output,
    query_grad,
    key_grad,
    value_grad,
    output_grad,
    gate_grad,
    up_grad,
    down_grad,
):
    shards, narrow, block = grads.shape
    depth = inputs.shape[1]
    values = inputs[...].astype(f32)
    every_weight = weights[...].reshape(shards * narrow, depth)
    back = dot(grads[...].reshape(shards * narrow, block), every_weight, 0, 0)
    root = lax.rsqrt(jnp.mean(values * values, axis=-1, keepdims=True) + EPSILON)
    scaled = first_gain[...].astype(f32).reshape(1, depth) * back
    mean = jnp.mean(scaled * values, axis=-1, keepdims=True)
    result = hidden_back[...] + root * scaled
    input_grad[...] = result - values * (root * root * root * mean)
    layer_output[...] = layer_in[...]

    @pl.when(pl.program_id(0) == 0)
    def _():
        features, units = query_grad.shape[1], gate_grad.shape[1]
        query_grad[...] = narrow_total[:, :features]
        key_grad[...] = narrow_total[:, features : 2 * features]
        value_grad[...] = narrow_total[:, 2 * features : 3 * features]
        gate_grad[...] = wide_total[:, :units]
        up_grad[...] = wide_total[:, units : 2 * units]
        down_grad[...] = wide_total[:, 2 * units :]
        output_grad[...] = narrow_total[:, 3 * features :].T


def vmem():
    return pl.BlockSpec(memory_space=pltpu.VMEM)


def anywhere():
    return pl.BlockSpec(memory_space=pl.ANY)


def body(groups, shards, *arguments):
    (
        patches,
        attention_gain,
        query_weight,
        key_weight,
        value_weight,
        output_weight,
        feedforward_gain,
        gate_weight,
        up_weight,
        down_weight,
        cotangent,
        grid_extent,
    ) = arguments
    rows, depth = patches.shape
    features, units = query_weight.shape[1], gate_weight.shape[1]
    heads = shards * features // HEAD
    piece = depth // GROUP
    wide, narrow = 3 * units, 3 * features
    mixed = narrow + features

    shape = jax.ShapeDtypeStruct
    kinds = Gather.KINDS
    dma = pltpu.SemaphoreType.DMA
    (
        layer_output,
        _,
        grads,
        weights,
        hidden_back,
        wide_total,
        narrow_total,
        gains_total,
    ) = pl.pallas_call(
        main_kernel,
        name="layer",
        out_shape=(
            shape((rows, depth), bf16),
            shape((heads, rows, rows), bf16),
            shape((shards, narrow, rows), bf16),
            shape((shards, 3, features, depth), bf16),
            shape((rows, depth), f32),
            shape((piece, wide), f32),
            shape((piece, mixed), f32),
            shape((piece, 128), f32),
        ),
        in_specs=[pl.BlockSpec(memory_space=pltpu.SMEM)] + [vmem()] * 3 + [anywhere()] * 8,
        out_specs=(anywhere(),) * 5 + (vmem(),) * 3,
        scratch_shapes=[
            pltpu.VMEM((shards, 3, features, depth), bf16),
            pltpu.VMEM((shards, features, depth), bf16),
            pltpu.VMEM((shards, depth, units), bf16),
            pltpu.VMEM((shards, depth, units), bf16),
            pltpu.VMEM((shards, units, depth), bf16),
            pltpu.VMEM((shards, narrow, rows), bf16),
            pltpu.VMEM((depth, rows), bf16),
            pltpu.VMEM((rows, depth), bf16),
            pltpu.VMEM((rows, depth), bf16),
            pltpu.VMEM((rows, depth), bf16),
            pltpu.VMEM((rows, depth), f32),
            pltpu.VMEM((heads, 1, rows), f32),
            pltpu.VMEM((heads, 1, rows), f32),
            pltpu.VMEM((depth, rows), bf16),
            pltpu.VMEM((4, 2, piece, wide), bf16),
            pltpu.VMEM((4, 2, piece, mixed), bf16),
            pltpu.VMEM((4, piece, wide), bf16),
            pltpu.VMEM((3, piece, wide), bf16),
            pltpu.VMEM((4, piece, mixed), bf16),
            pltpu.VMEM((3, piece, mixed), bf16),
            pltpu.VMEM((piece, 128), f32),
            pltpu.VMEM((3, piece, 128), f32),
            pltpu.VMEM((depth, narrow), bf16),
            dma((8,)),
            dma((2,)),
            dma((3,)),
            dma((shards,)),
            dma((2, 4)),
            dma((2, 4)),
            dma((2, shards)),
            dma((kinds, shards)),
            dma((kinds, shards)),
            dma((kinds, shards, 4)),
            dma((kinds, shards, 4)),
            dma((kinds, shards, 4)),
            dma((kinds, shards, 4)),
        ],
        compiler_params=pltpu.CompilerParams(
            collective_id=0, has_side_effects=True, vmem_limit_bytes=VMEM_LIMIT
        ),
    )(
        grid_extent,
        patches,
        attention_gain,
        feedforward_gain,
        cotangent,
        query_weight.T,
        key_weight.T,
        value_weight.T,
        output_weight,
        gate_weight,
        up_weight,
        down_weight,
    )

    block = 256

    def whole(*dims):
        return pl.BlockSpec(dims, lambda i: (0,) * len(dims))

    by_rows = pl.BlockSpec((block, depth), lambda i: (i, 0))
    small = [(piece, features)] * 3 + [(features, piece)] + [(piece, units)] * 3
    input_grad, layer_output, *small_grads = pl.pallas_call(
        close_kernel,
        name="close",
        grid=(rows // block,),
        out_shape=[shape((rows, depth), f32), shape((rows, depth), bf16)]
        + [shape(dims, f32) for dims in small],
        in_specs=[
            pl.BlockSpec((shards, narrow, block), lambda i: (0, 0, i)),
            whole(shards, 3, features, depth),
            by_rows,
            by_rows,
            whole(depth),
            by_rows,
            whole(piece, wide),
            whole(piece, mixed),
        ],
        out_specs=[by_rows, by_rows] + [whole(*dims) for dims in small],
        compiler_params=pltpu.CompilerParams(vmem_limit_bytes=VMEM_LIMIT),
    )(grads, weights, hidden_back, patches, attention_gain, layer_output, wide_total, narrow_total)

    index = lax.axis_index("dp")
    gains_total = gains_total[:, :2]
    if groups > 1:

        def spread(block, turned=False):
            block = block.T if turned else block
            whole = jnp.zeros((depth, block.shape[1]), f32)
            whole = lax.dynamic_update_slice(whole, block, ((index % GROUP) * piece, 0))
            own = lax.psum_scatter(whole, "dp", scatter_dimension=0, tiled=True)
            return own.T if turned else own

        small_grads = [spread(grad, i == 3) for i, grad in enumerate(small_grads)]
        gains_total = spread(gains_total)
    kept = depth // (groups * GROUP)

    def gain_grad(column, gain):
        own = lax.dynamic_slice_in_dim(gain.astype(f32), index * kept, kept)
        return gains_total[:, column] / own

    query_grad, key_grad, value_grad, output_grad, gate_grad, up_grad, down_grad = small_grads
    return (
        layer_output,
        input_grad,
        gain_grad(0, attention_gain),
        query_grad,
        key_grad,
        value_grad,
        output_grad,
        gain_grad(1, feedforward_gain),
        gate_grad,
        up_grad,
        down_grad.T,
    )


def solution(mesh):
    placed = (
        P("dp", None),
        P(),
        P(None, "mp"),
        P(None, "mp"),
        P(None, "mp"),
        P("mp", None),
        P(),
        P(None, "mp"),
        P(None, "mp"),
        P("mp", None),
        P("dp", None),
        P("dp", None),
    )
    return jax.shard_map(
        functools.partial(body, mesh.shape["dp"] // GROUP, mesh.shape["mp"]),
        mesh=mesh,
        in_specs=placed,
        out_specs=(
            P("dp", None),
            P("dp", None),
            P("dp"),
            P("dp", "mp"),
            P("dp", "mp"),
            P("dp", "mp"),
            P("mp", "dp"),
            P("dp"),
            P("dp", "mp"),
            P("dp", "mp"),
            P("mp", "dp"),
        ),
        check_vma=False,
    )
```

profile of v0, /device:TPU:0, one launch (start us, length us, event | category | flops | bytes accessed | tf_op | source)
XLA Modules:
  0.0 133.8 jit_solution(16213716697012067430)
XLA Ops:
  0.6 121.2 %layer.1 = (bf16[1024,768]{1,0:T(8,128)(2,1)}, bf16[12,1024,1024]{2,1,0:T(8,128)(2,1)}, bf16[4,576,1024]{2,1,0:T(8,128)(2,1)}, bf16[4,3,192,768]{3,2,1,0:T(8,128...) custom-call(s32[1,2]{1,0:T(1,128)} %extent.1, ...), custom_call_target="tpu_custom_call" | custom-call | tf_op jit(solution)/shard_map/layer/pallas_call | solution.py:787
  121.8 0.0 copy-start
  121.9 0.0 copy-start.1
  121.9 0.0 copy-start.2
  121.9 11.1 %close.1 = (f32[1024,768]{1,0:T(8,128)}, bf16[1024,768]{1,0:T(8,128)(2,1)}, f32[96,192]{1,0:T(8,128)}, f32[96,192]{1,0:T(8,128)}, f32[96,192]{1,0:T(8,128)}, /*i...) custom-call(bf16[4,576,1024]{2,1,0:T(8,128)(2,1)} %get-tuple-element.27.grads, ...), custom_call_target="tpu_custom_call" | custom-call | tf_op jit(solution)/shard_map/close/pallas_call | solution.py:865
  132.9 0.0 copy-done
  133.0 0.2 slice_reduce_fusion
  133.1 0.0 copy-done.1
  133.2 0.0 copy-done.2
  133.2 0.6 dynamic-slice_divide_fusion
  (2 shorter events, 0.0 us)
Async XLA Ops:
  121.8 11.1 %copy-start = (f32[96,128]{1,0:T(8,128)S(1)}, f32[96,128]{1,0:T(8,128)}, u32[]{:S(2)}) copy-start(f32[96,128]{1,0:T(8,128)} %get-tuple-element.35) | copy-start | bytes 147460
  121.9 11.3 %copy-start.1 = (bf16[768]{0:T(1024)(128)(2,1)S(1)}, bf16[768]{0:T(1024)(128)(2,1)}, u32[]{:S(2)}) copy-start(bf16[768]{0:T(1024)(128)(2,1)} %first_gain.3) | copy-start | bytes 4612
  121.9 11.3 %copy-start.2 = (bf16[768]{0:T(1024)(128)(2,1)S(1)}, bf16[768]{0:T(1024)(128)(2,1)}, u32[]{:S(2)}) copy-start(bf16[768]{0:T(1024)(128)(2,1)} %second_gain.1) | copy-start | bytes 4612
where the time goes:
time: 134 us
  Pallas kernels  132 us (99%)
    pallas_call x1, Pallas kernels, body(): pl.pallas_call(main_kernel, name='layer', out_shape=(shape((rows, depth),...  121 us
    pallas_call x1, Pallas kernels, body(): pl.pallas_call(close_kernel, name='close', grid=(rows // block,), out_sha...  11.1 us

commit v1 on v0

--- a/solution.py
+++ b/solution.py
@@ -135,7 +135,7 @@
             piece = self.place(kind, flip(self.mp, k), flip(self.chip, j), 1 - self.core)
             self.arrived(piece, send_c.at[kind, k, j], recv_c.at[kind, k, j])
 
-    def schedule(self, jobs, window=8, start=3.0, pace=3.2, lags=(6.0, 12.0, 14.0)):
+    def schedule(self, jobs, window=8, start=3.0, pace=3.0, lags=(6.0, 12.0, 14.0)):
         for job in jobs[:window]:
             self.start(self.along_mp, *job)
 

time: 134 us -> 132 us (0.985)
    pallas_call x1, Pallas kernels: 121 us -> 120 us  [body(): pl.pallas_call(main_kernel, name='layer', out_shape=(shape((rows, depth),...]
where the time goes in v1:
time: 132 us
  Pallas kernels  131 us (99%)
    pallas_call x1, Pallas kernels, body(): pl.pallas_call(main_kernel, name='layer', out_shape=(shape((rows, depth),...  120 us
    pallas_call x1, Pallas kernels, body(): pl.pallas_call(close_kernel, name='close', grid=(rows // block,), out_sha...  11.1 us

profile of v1, /device:TPU:0, one launch (start us, length us, event | category | flops | bytes accessed | tf_op | source)
XLA Modules:
  0.0 132.1 jit_solution(9218330398257356793)
XLA Ops:
  0.6 119.5 %layer.1 = (bf16[1024,768]{1,0:T(8,128)(2,1)}, bf16[12,1024,1024]{2,1,0:T(8,128)(2,1)}, bf16[4,576,1024]{2,1,0:T(8,128)(2,1)}, bf16[4,3,192,768]{3,2,1,0:T(8,128...) custom-call(s32[1,2]{1,0:T(1,128)} %extent.1, ...), custom_call_target="tpu_custom_call" | custom-call | tf_op jit(solution)/shard_map/layer/pallas_call | solution.py:787
  120.2 0.0 copy-start
  120.2 0.0 copy-start.1
  120.2 0.0 copy-start.2
  120.2 11.1 %close.1 = (f32[1024,768]{1,0:T(8,128)}, bf16[1024,768]{1,0:T(8,128)(2,1)}, f32[96,192]{1,0:T(8,128)}, f32[96,192]{1,0:T(8,128)}, f32[96,192]{1,0:T(8,128)}, /*i...) custom-call(bf16[4,576,1024]{2,1,0:T(8,128)(2,1)} %get-tuple-element.27.grads, ...), custom_call_target="tpu_custom_call" | custom-call | tf_op jit(solution)/shard_map/close/pallas_call | solution.py:865
  131.3 0.0 copy-done
  131.3 0.2 slice_reduce_fusion
  131.5 0.0 copy-done.1
  131.5 0.0 copy-done.2
  131.5 0.6 dynamic-slice_divide_fusion
  (2 shorter events, 0.0 us)
Async XLA Ops:
  120.2 11.1 %copy-start = (f32[96,128]{1,0:T(8,128)S(1)}, f32[96,128]{1,0:T(8,128)}, u32[]{:S(2)}) copy-start(f32[96,128]{1,0:T(8,128)} %get-tuple-element.35) | copy-start | bytes 147460
  120.2 11.3 %copy-start.1 = (bf16[768]{0:T(1024)(128)(2,1)S(1)}, bf16[768]{0:T(1024)(128)(2,1)}, u32[]{:S(2)}) copy-start(bf16[768]{0:T(1024)(128)(2,1)} %first_gain.3) | copy-start | bytes 4612
  120.2 11.3 %copy-start.2 = (bf16[768]{0:T(1024)(128)(2,1)S(1)}, bf16[768]{0:T(1024)(128)(2,1)}, u32[]{:S(2)}) copy-start(bf16[768]{0:T(1024)(128)(2,1)} %second_gain.1) | copy-start | bytes 4612

commit v2 on v1

--- a/solution.py
+++ b/solution.py
@@ -173,7 +173,7 @@
 def project(weights_ref, normed_ref, out_ref, shard):
     parts, features, depth = weights_ref.shape[1:]
     rows = normed_ref.shape[0]
-    block = 512
+    block = 1024
 
     def step(i, _):
         at = pl.ds(aligned(i * block, block), block)

time: 132 us -> 132 us (level)
  no operation moved by 1% of the time
where the time goes in v2:
time: 132 us
  Pallas kernels  130 us (98%)
    pallas_call x1, Pallas kernels, body(): pl.pallas_call(main_kernel, name='layer', out_shape=(shape((rows, depth),...  119 us
    pallas_call x1, Pallas kernels, body(): pl.pallas_call(close_kernel, name='close', grid=(rows // block,), out_sha...  11.1 us

profile of v2, /device:TPU:0, one launch (start us, length us, event | category | flops | bytes accessed | tf_op | source)
XLA Modules:
  0.0 132.0 jit_solution(12389697941491872595)
XLA Ops:
  0.6 119.4 %layer.1 = (bf16[1024,768]{1,0:T(8,128)(2,1)}, bf16[12,1024,1024]{2,1,0:T(8,128)(2,1)}, bf16[4,576,1024]{2,1,0:T(8,128)(2,1)}, bf16[4,3,192,768]{3,2,1,0:T(8,128...) custom-call(s32[1,2]{1,0:T(1,128)} %extent.1, ...), custom_call_target="tpu_custom_call" | custom-call | tf_op jit(solution)/shard_map/layer/pallas_call | solution.py:787
  120.1 0.0 copy-start
  120.1 0.0 copy-start.1
  120.1 0.0 copy-start.2
  120.1 11.1 %close.1 = (f32[1024,768]{1,0:T(8,128)}, bf16[1024,768]{1,0:T(8,128)(2,1)}, f32[96,192]{1,0:T(8,128)}, f32[96,192]{1,0:T(8,128)}, f32[96,192]{1,0:T(8,128)}, /*i...) custom-call(bf16[4,576,1024]{2,1,0:T(8,128)(2,1)} %get-tuple-element.27.grads, ...), custom_call_target="tpu_custom_call" | custom-call | tf_op jit(solution)/shard_map/close/pallas_call | solution.py:865
  131.1 0.0 copy-done
  131.2 0.2 slice_reduce_fusion
  131.3 0.0 copy-done.1
  131.4 0.0 copy-done.2
  131.4 0.6 dynamic-slice_divide_fusion
  (2 shorter events, 0.0 us)
Async XLA Ops:
  120.1 11.1 %copy-start = (f32[96,128]{1,0:T(8,128)S(1)}, f32[96,128]{1,0:T(8,128)}, u32[]{:S(2)}) copy-start(f32[96,128]{1,0:T(8,128)} %get-tuple-element.35) | copy-start | bytes 147460
  120.1 11.3 %copy-start.1 = (bf16[768]{0:T(1024)(128)(2,1)S(1)}, bf16[768]{0:T(1024)(128)(2,1)}, u32[]{:S(2)}) copy-start(bf16[768]{0:T(1024)(128)(2,1)} %first_gain.3) | copy-start | bytes 4612
  120.1 11.3 %copy-start.2 = (bf16[768]{0:T(1024)(128)(2,1)S(1)}, bf16[768]{0:T(1024)(128)(2,1)}, u32[]{:S(2)}) copy-start(bf16[768]{0:T(1024)(128)(2,1)} %second_gain.1) | copy-start | bytes 4612

commit v3 on v2

--- a/solution.py
+++ b/solution.py
@@ -187,7 +187,7 @@
 def attend(qkv_ref, shard, head, count, probs_ref, context_ref, scale_ref, scores, keys, local_heads, pause):
     rows = qkv_ref.shape[2]
     width = local_heads * HEAD
-    block, chunk, group = 256, 128, 64
+    block, chunk, group = 256, 128, 128
     at = pl.ds(aligned(head * HEAD, HEAD), HEAD)
     number = shard * local_heads + head
     context_at = pl.ds(aligned(number * HEAD, HEAD), HEAD)

time: 132 us -> 132 us (level)
  no operation moved by 1% of the time
where the time goes in v3:
time: 132 us
  Pallas kernels  130 us (98%)
    pallas_call x1, Pallas kernels, body(): pl.pallas_call(main_kernel, name='layer', out_shape=(shape((rows, depth),...  119 us
    pallas_call x1, Pallas kernels, body(): pl.pallas_call(close_kernel, name='close', grid=(rows // block,), out_sha...  11.1 us

profile of v3, /device:TPU:0, one launch (start us, length us, event | category | flops | bytes accessed | tf_op | source)
XLA Modules:
  0.0 132.0 jit_solution(12079910283479537276)
XLA Ops:
  0.6 119.4 %layer.1 = (bf16[1024,768]{1,0:T(8,128)(2,1)}, bf16[12,1024,1024]{2,1,0:T(8,128)(2,1)}, bf16[4,576,1024]{2,1,0:T(8,128)(2,1)}, bf16[4,3,192,768]{3,2,1,0:T(8,128...) custom-call(s32[1,2]{1,0:T(1,128)} %extent.1, ...), custom_call_target="tpu_custom_call" | custom-call | tf_op jit(solution)/shard_map/layer/pallas_call | solution.py:787
  120.1 0.0 copy-start
  120.1 0.0 copy-start.1
  120.1 0.0 copy-start.2
  120.1 11.1 %close.1 = (f32[1024,768]{1,0:T(8,128)}, bf16[1024,768]{1,0:T(8,128)(2,1)}, f32[96,192]{1,0:T(8,128)}, f32[96,192]{1,0:T(8,128)}, f32[96,192]{1,0:T(8,128)}, /*i...) custom-call(bf16[4,576,1024]{2,1,0:T(8,128)(2,1)} %get-tuple-element.27.grads, ...), custom_call_target="tpu_custom_call" | custom-call | tf_op jit(solution)/shard_map/close/pallas_call | solution.py:865
  131.2 0.0 copy-done
  131.2 0.2 slice_reduce_fusion
  131.3 0.0 copy-done.1
  131.4 0.0 copy-done.2
  131.4 0.6 dynamic-slice_divide_fusion
  (2 shorter events, 0.0 us)
Async XLA Ops:
  120.1 11.1 %copy-start = (f32[96,128]{1,0:T(8,128)S(1)}, f32[96,128]{1,0:T(8,128)}, u32[]{:S(2)}) copy-start(f32[96,128]{1,0:T(8,128)} %get-tuple-element.35) | copy-start | bytes 147460
  120.1 11.3 %copy-start.1 = (bf16[768]{0:T(1024)(128)(2,1)S(1)}, bf16[768]{0:T(1024)(128)(2,1)}, u32[]{:S(2)}) copy-start(bf16[768]{0:T(1024)(128)(2,1)} %first_gain.3) | copy-start | bytes 4612
  120.1 11.3 %copy-start.2 = (bf16[768]{0:T(1024)(128)(2,1)S(1)}, bf16[768]{0:T(1024)(128)(2,1)}, u32[]{:S(2)}) copy-start(bf16[768]{0:T(1024)(128)(2,1)} %second_gain.1) | copy-start | bytes 4612
